TPU v7x, 32 devices: a whole 2x2x4 slice. The times are simulated.
32 devices in a mesh: trial: 2 (over y), fsdp: 8 (over z, x), tensor: 2 (over core).
Axes of the slice: x: 2, y: 2, z: 4, core: 2. Of those that a mesh axis runs over, the one named last changes fastest.
Arguments:
- tokens: bfloat16 [4096, 4096], P(('trial', 'fsdp'), 'tensor'), parts along dimension 0, may hold values from -110 to 110
- norm_gain: float32 [4096], replicated, may hold values from 0.25 to 1.75
- grow_width: bfloat16 [4096, 2048], P('fsdp'), may hold values from -0.09375 to 0.09375
- old_value: bfloat16 [2048, 1024], P('fsdp', 'tensor'), may hold values from -0.125 to 0.125
- grow_head: bfloat16 [2048, 1024], P('tensor', 'fsdp'), may hold values from -0.1875 to 0.1875
- cotangent: bfloat16 [4096, 2048], P(('trial', 'fsdp'), 'tensor'), parts along dimension 0, may hold values from -6 to 6
Outputs:
- grown_value: bfloat16 [8192, 1024], P(('trial', 'fsdp'), 'tensor'), parts along dimension 0
- value_out: bfloat16 [4096, 2048], P(('trial', 'fsdp'), 'tensor'), parts along dimension 0
- head_grad: float32 [2048, 2048], P(('trial', 'fsdp'), 'tensor'), parts along dimension 0
There are 2 independent parts, one for each index of `trial`. A program takes and returns all parts, laid end to end along the dimension named above; an argument that names none is the same for every part. Nothing has to cross between parts.
All inputs are finite; a program needn't handle non-finite values.
Results may differ from a plain program's by a relative error of at most 0.0064.
Values may be sent and summed in bfloat16 or wider, within the bound.
A program may use at most 64 MiB of HBM per device.

v0:
```python
import math

import jax
import jax.numpy as jnp
from jax import lax
from jax.sharding import PartitionSpec as P


def per_device(tokens, norm_gain, grow_width, old_value, grow_head, cotangent):
    whole = lax.all_gather(tokens, "tensor", axis=1, tiled=True)
    widened = whole.astype(jnp.float32)
    meansq = jnp.mean(widened * widened, axis=-1, keepdims=True)
    normed = (widened * lax.rsqrt(meansq + 1e-05) * norm_gain).astype(jnp.bfloat16)
    old_rows = lax.all_gather(old_value, "tensor", axis=1, tiled=True)
    old_all = lax.all_gather(old_rows, "fsdp", axis=0, tiled=True)
    grown_slab = jnp.dot(grow_width, old_all, preferred_element_type=jnp.float32).astype(
        jnp.bfloat16
    )
    grown_full = lax.all_gather(grown_slab, "fsdp", axis=0, tiled=True)
    mixed = jnp.dot(normed, grown_full, preferred_element_type=jnp.float32).astype(jnp.bfloat16)
    half_width = old_all.shape[1] // lax.axis_size("tensor")
    grown_value = lax.dynamic_slice_in_dim(
        grown_slab, lax.axis_index("tensor") * half_width, half_width, 1
    )
    head_all = lax.all_gather(grow_head, "fsdp", axis=1, tiled=True)
    value_out = lax.dot_general(
        mixed, head_all, (((1,), (1,)), ((), ())), preferred_element_type=jnp.float32
    ).astype(jnp.bfloat16)
    summed = lax.psum_scatter(
        lax.dot_general(
            mixed, cotangent, (((0,), (0,)), ((), ())), preferred_element_type=jnp.float32
        ),
        "fsdp",
        scatter_dimension=0,
        tiled=True,
    )
    head_grad = summed * (1.0 / math.sqrt(tokens.shape[0] * lax.axis_size("fsdp")))
    return (grown_value, value_out, head_grad)


def solution(mesh):
    return jax.shard_map(
        per_device,
        mesh=mesh,
        in_specs=(
            P(("trial", "fsdp"), "tensor"),
            P(),
            P("fsdp", None),
            P("fsdp", "tensor"),
            P("tensor", "fsdp"),
            P(("trial", "fsdp"), "tensor"),
        ),
        out_specs=(
            P(("trial", "fsdp"), "tensor"),
            P(("trial", "fsdp"), "tensor"),
            P(("trial", "fsdp"), "tensor"),
        ),
        check_vma=False,
    )
```

profile of v0, /device:TPU:0, one launch (start us, length us, event | category | flops | bytes accessed | tf_op | source)
XLA Modules:
  0.0 375.4 jit_solution(16384810196821062314)
XLA Ops:
  7.2 0.0 copy-start
  7.2 0.0 all-gather.5.cloned.1.call-start
  7.2 4.3 %all_gather.15 = bf16[256,1024]{1,0:T(8,128)(2,1)} all-gather(bf16[256,512]{1,0:T(8,128)(2,1)} %param.9), channel_id=1, replica_groups=mesh['trial'=2,'fsdp'=8,'tensor'=2] {'tensor'}, dimensions={1}, use_global_device_ids=true | all-gather | bytes 786432 | tf_op jit(solution)/shard_map/all_gather | solution.py:14
  11.6 0.0 all-gather.5.cloned.1.call-update
  11.6 0.0 all-gather.7.cloned.1.call-start
  11.6 0.7 all-gather.7.cloned.1.call-update
  12.3 0.0 copy-start.4
  12.3 0.0 all-gather.9.cloned.1.call-start
  12.4 75.1 %all-gather.5.cloned.1.call-done = bf16[2048,1024]{1,0:T(8,128)(2,1)} async-done(((bf16[256,1024]{1,0:T(8,128)(2,1)}), bf16[2048,1024]{1,0:T(8,128)(2,1)}) %all-gather.5.cloned.1.call-update) | async-done | bytes 4194320 | tf_op jit(solution)/shard_map/all_gather | solution.py:15
  87.5 0.0 copy-done
  87.5 5.6 %convolution_convert_fusion = bf16[512,1024]{1,0:T(8,128)(2,1)} fusion(bf16[512,2048]{1,0:T(8,128)(2,1)S(1)} %copy-done, bf16[2048,1024]{1,0:T(8,128)(2,1)} %all-gather.5.cloned.1.call-done), kind=kOutput, calls=%fused_computation.8 | convolution fusion | flops 2148007936 | bytes 7340032 | tf_op jit(solution)/shard_map/dot_general | solution.py:16
  93.1 0.0 all-gather.9.cloned.1.call-update
  93.1 0.0 all-gather.11.cloned.1.call-start
  93.2 0.5 all-gather.11.cloned.1.call-update
  93.7 0.0 reduce-scatter.2.cloned.1.call-start
  93.7 4.2 %all-gather.7.cloned.1.call-done = bf16[256,4096]{1,0:T(8,128)(2,1)} async-done(((bf16[256,2048]{1,0:T(8,128)(2,1)}), bf16[256,4096]{1,0:T(8,128)(2,1)}) %all-gather.7.cloned.1.call-update) | async-done | bytes 2097168 | tf_op jit(solution)/shard_map/all_gather | solution.py:10
  97.9 2.1 fusion
  100.0 0.0 copy-start.3
  100.0 126.2 %all-gather.9.cloned.1.call-done = bf16[4096,1024]{1,0:T(8,128)(2,1)} async-done(((bf16[512,1024]{1,0:T(8,128)(2,1)}), bf16[4096,1024]{1,0:T(8,128)(2,1)}) %all-gather.9.cloned.1.call-update) | async-done | bytes 8388624 | tf_op jit(solution)/shard_map/all_gather | solution.py:19
  226.2 0.0 copy-done.4
  226.2 6.4 %fusion.7 = bf16[256,1024]{1,0:T(8,128)(2,1)S(1)} fusion(bf16[4096,1024]{1,0:T(8,128)(2,1)} %all-gather.9.cloned.1.call-done, bf16[256,4096]{1,0:T(8,128)(2,1)} %all-gather.7.cloned.1.call-done, f32[4096]{0:T(1024)S(1)} %copy-done.4, f32[256]{0:T(256)S(1)} %add_rsqrt_fusion), kind=kOutput, calls=%fused_computation.9 | convolution fusion | flops 2151940096 | bytes 11027456 | tf_op jit(solution)/shard_map/dot_general | solution.py:20
  232.6 0.0 copy-start.2
  232.6 0.8 copy-done.2
  233.4 0.0 copy-done.3
  233.4 2.7 fusion.10
  236.1 0.0 copy-start.1
  236.1 0.0 reduce-scatter.2.cloned.1.call-update
  236.1 1.2 copy-done.1
  237.3 0.8 constant_dynamic-slice_fusion
  238.2 39.2 %all-gather.11.cloned.1.call-done = bf16[1024,1024]{1,0:T(8,128)(2,1)} async-done(((bf16[1024,128]{1,0:T(8,128)(2,1)}), bf16[1024,1024]{1,0:T(8,128)(2,1)}) %all-gather.11.cloned.1.call-update) | async-done | bytes 2097168 | tf_op jit(solution)/shard_map/all_gather | solution.py:25
  277.4 3.3 convolution_convert_fusion.1
  280.7 86.3 %reduce-scatter.2.cloned.1.call-done = f32[128,1024]{1,0:T(8,128)} async-done(((f32[1024,1024]{1,0:T(8,128)}), f32[128,1024]{1,0:T(8,128)}) %reduce-scatter.2.cloned.1.call-update) | async-done | bytes 524304 | tf_op jit(solution)/shard_map/reduce_scatter | solution.py:29
  367.0 1.9 broadcast_multiply_fusion
  (1 shorter events, 0.0 us)
Async XLA Ops:
  7.2 80.4 %copy-start = (bf16[512,2048]{1,0:T(8,128)(2,1)S(1)}, bf16[512,2048]{1,0:T(8,128)(2,1)}, u32[]{:S(2)}) copy-start(bf16[512,2048]{1,0:T(8,128)(2,1)} %param.8) | copy-start | bytes 6291460
  7.2 80.3 %all-gather.5.cloned.1.call-start = ((), (), s32[]{:S(2)}) async-start(), calls=%async_computation.1 | async-start | bytes 4718592 | tf_op jit(solution)/shard_map/all_gather | solution.py:15
  11.6 86.4 %all-gather.7.cloned.1.call-start = ((), (), s32[]{:S(2)}) async-start(), calls=%async_computation.2 | async-start | bytes 3145728 | tf_op jit(solution)/shard_map/all_gather | solution.py:10
  12.3 213.9 %copy-start.4 = (f32[4096]{0:T(1024)S(1)}, f32[4096]{0:T(1024)}, u32[]{:S(2)}) copy-start(f32[4096]{0:T(1024)} %param.7) | copy-start | bytes 49156
  12.3 213.9 %all-gather.9.cloned.1.call-start = ((), (), s32[]{:S(2)}) async-start(), calls=%async_computation.3 | async-start | bytes 9437184 | tf_op jit(solution)/shard_map/all_gather | solution.py:19
  93.1 184.3 %all-gather.11.cloned.1.call-start = ((), (), s32[]{:S(2)}) async-start(), calls=%async_computation.4 | async-start | bytes 2359296 | tf_op jit(solution)/shard_map/all_gather | solution.py:25
  93.7 273.3 %reduce-scatter.2.cloned.1.call-start = ((), (), s32[]{:S(2)}) async-start(), calls=%async_computation.5 | async-start | bytes 4718592 | tf_op jit(solution)/shard_map/reduce_scatter | solution.py:29
  100.0 133.4 %copy-start.3 = (bf16[256,1024]{1,0:T(8,128)(2,1)S(1)}, bf16[256,1024]{1,0:T(8,128)(2,1)}, u32[]{:S(2)}) copy-start(bf16[256,1024]{1,0:T(8,128)(2,1)} %param.11) | copy-start | bytes 1572868
  232.6 0.8 copy-start.2
  236.1 1.2 copy-start.1
Sparse Core Ops, SparseCore 0:
  11.7 75.7 all-gather.4
  89.1 8.8 all-gather.6
  100.1 126.0 all-gather.8
  228.1 49.2 all-gather.10
  280.9 86.0 reduce-scatter.1
where the time goes:
time: 376 us; the launch traced here: 375 us
  waiting for transfers between devices  332 us (88%)
  matrix products  18 us (5%)
  between operations  13.8 us (4%)
  blocking collectives  4.33 us (1%)
  other arithmetic  3.98 us (1%)
    all_gather x1, waiting for transfers between devices, per_device(): grown_full = lax.all_gather(grown_slab, 'fsdp', axis=0, tiled=True)  126 us
    reduce_scatter x1, waiting for transfers between devices, per_device(): lax.psum_scatter(lax.dot_general(mixed, cotangent, (((0,), (0,)), ((), ()...  86.3 us
    all_gather x1, waiting for transfers between devices, per_device(): old_all = lax.all_gather(old_rows, 'fsdp', axis=0, tiled=True)  75.1 us
    all_gather x1, waiting for transfers between devices, per_device(): head_all = lax.all_gather(grow_head, 'fsdp', axis=1, tiled=True)  39.2 us
  transfers between devices with their start and end apart: 5, of which 5 were waited for; matrix products, arithmetic and copies ran while one was open for 6% of the time, Pallas kernels for 0%

commit v1 on v0

v1 whole, which is shorter than its diff:
```python
import math

import jax
import jax.numpy as jnp
from jax import lax
from jax.sharding import PartitionSpec as P


def per_device(tokens, norm_gain, grow_width, old_value, grow_head, cotangent):
    shards = lax.axis_size("fsdp")
    old_half = lax.all_gather(old_value, "fsdp", axis=0, tiled=True)
    grown_value = jnp.dot(grow_width, old_half, preferred_element_type=jnp.float32).astype(
        jnp.bfloat16
    )
    grown_half = lax.all_gather(grown_value, "fsdp", axis=0, tiled=True)
    whole = lax.all_gather(tokens, "tensor", axis=1, tiled=True)
    widened = whole.astype(jnp.float32)
    meansq = jnp.mean(widened * widened, axis=-1, keepdims=True)
    normed = (widened * lax.rsqrt(meansq + 1e-05) * norm_gain).astype(jnp.bfloat16)
    mixed_half = jnp.dot(normed, grown_half, preferred_element_type=jnp.float32).astype(
        jnp.bfloat16
    )
    mixed = lax.all_gather(mixed_half, "tensor", axis=1, tiled=True)
    head_all = lax.all_gather(grow_head, "fsdp", axis=1, tiled=True)
    value_out = lax.dot_general(
        mixed, head_all, (((1,), (1,)), ((), ())), preferred_element_type=jnp.float32
    ).astype(jnp.bfloat16)
    partial = lax.dot_general(
        mixed, cotangent, (((0,), (0,)), ((), ())), preferred_element_type=jnp.float32
    ).astype(jnp.bfloat16)
    partial = partial.reshape(shards, partial.shape[0] // shards, partial.shape[1])
    parts = lax.all_to_all(partial, "fsdp", split_axis=0, concat_axis=0, tiled=True)
    summed = jnp.sum(parts.astype(jnp.float32), axis=0)
    head_grad = summed * (1.0 / math.sqrt(tokens.shape[0] * shards))
    return (grown_value, value_out, head_grad)


def solution(mesh):
    return jax.shard_map(
        per_device,
        mesh=mesh,
        in_specs=(
            P(("trial", "fsdp"), "tensor"),
            P(),
            P("fsdp", None),
            P("fsdp", "tensor"),
            P("tensor", "fsdp"),
            P(("trial", "fsdp"), "tensor"),
        ),
        out_specs=(
            P(("trial", "fsdp"), "tensor"),
            P(("trial", "fsdp"), "tensor"),
            P(("trial", "fsdp"), "tensor"),
        ),
        check_vma=False,
    )
```

time: 376 us -> 246 us (0.65)
  waiting for transfers between devices: 332 us -> 207 us
  matrix products: 18 us -> 13 us
  starting transfers between devices: 0.2 us -> 4.51 us
    reduce_scatter x1 -> x0, waiting for transfers between devices: 86.3 us -> none  [per_device(): lax.psum_scatter(lax.dot_general(mixed, cotangent, (((0,), (0,)), ((), ()...]
    all_gather x2, waiting for transfers between devices: 201 us -> 129 us  [the longest x1 75.2 us: per_device(): grown_half = lax.all_gather(grown_value, 'fsdp', axis=0, tiled=True)]
    all_gather x1, waiting for transfers between devices: 39.2 us -> 69.8 us  [per_device(): head_all = lax.all_gather(grow_head, 'fsdp', axis=1, tiled=True)]
    all_to_all x0 -> x1, starting transfers between devices: none -> 4.35 us  [per_device(): lax.all_to_all(partial, 'fsdp', split_axis=0, concat_axis=0, tiled=True)]
    dot_general x2, matrix products: 12 us -> 7.76 us  [the longest x1 4.13 us: per_device(): jnp.dot(normed, grown_half, preferred_element_type=jnp.float32)]
  transfers between devices with their start and end apart: 5 -> 5, of which waited for: 5 -> 4; matrix products, arithmetic and copies ran while one was open for 6% -> 6% of each run, Pallas kernels for 0% -> 0%
where the time goes in v1:
time: 246 us; the launch traced here: 245 us
  waiting for transfers between devices  207 us (84%)
  between operations  13.8 us (6%)
  matrix products  13 us (5%)
  other arithmetic  4.95 us (2%)
  starting transfers between devices  4.51 us (2%)
    all_gather x1, waiting for transfers between devices, per_device(): grown_half = lax.all_gather(grown_value, 'fsdp', axis=0, tiled=True)  75.2 us
    all_gather x1, waiting for transfers between devices, per_device(): head_all = lax.all_gather(grow_head, 'fsdp', axis=1, tiled=True)  69.8 us
    all_gather x1, waiting for transfers between devices, per_device(): old_half = lax.all_gather(old_value, 'fsdp', axis=0, tiled=True)  53.4 us
    all_gather x1, waiting for transfers between devices, per_device(): whole = lax.all_gather(tokens, 'tensor', axis=1, tiled=True)  6.4 us
  transfers between devices with their start and end apart: 5, of which 4 were waited for; matrix products, arithmetic and copies ran while one was open for 6% of the time, Pallas kernels for 0%

profile of v1, /device:TPU:0, one launch (start us, length us, event | category | flops | bytes accessed | tf_op | source)
XLA Modules:
  0.0 245.2 jit_solution(13141053014122493109)
XLA Ops:
  7.2 0.0 copy-start
  7.2 0.0 all-gather.5.cloned.1.call-start
  7.2 0.7 all-gather.5.cloned.1.call-update
  7.9 0.0 all-gather.7.cloned.1.call-start
  8.0 0.7 all-gather.7.cloned.1.call-update
  8.7 0.0 all-gather.9.cloned.1.call-start
  8.7 53.4 %all-gather.5.cloned.1.call-done = bf16[2048,512]{1,0:T(8,128)(2,1)} async-done(((bf16[256,512]{1,0:T(8,128)(2,1)}), bf16[2048,512]{1,0:T(8,128)(2,1)}) %all-gather.5.cloned.1.call-update) | async-done | bytes 2097168 | tf_op jit(solution)/shard_map/all_gather | solution.py:11
  62.2 0.0 copy-done
  62.2 3.6 %convolution_convert_fusion.1 = bf16[512,512]{1,0:T(8,128)(2,1)} fusion(bf16[512,2048]{1,0:T(8,128)(2,1)S(1)} %copy-done, bf16[2048,512]{1,0:T(8,128)(2,1)} %all-gather.5.cloned.1.call-done), kind=kOutput, calls=%fused_computation.10 | convolution fusion | flops 1074003968 | bytes 4718592 | tf_op jit(solution)/shard_map/dot_general | solution.py:12
  65.8 0.0 copy-start.2
  65.8 0.0 all-gather.9.cloned.1.call-update
  65.8 0.0 all-gather.11.cloned.1.call-start
  65.9 0.5 all-gather.11.cloned.1.call-update
  66.4 6.4 %all-gather.7.cloned.1.call-done = bf16[256,4096]{1,0:T(8,128)(2,1)} async-done(((bf16[256,2048]{1,0:T(8,128)(2,1)}), bf16[256,4096]{1,0:T(8,128)(2,1)}) %all-gather.7.cloned.1.call-update) | async-done | bytes 2097168 | tf_op jit(solution)/shard_map/all_gather | solution.py:16
  72.8 2.1 fusion
  74.9 0.0 copy-start.1
  74.9 75.2 %all-gather.9.cloned.1.call-done = bf16[4096,512]{1,0:T(8,128)(2,1)} async-done(((bf16[512,512]{1,0:T(8,128)(2,1)}), bf16[4096,512]{1,0:T(8,128)(2,1)}) %all-gather.9.cloned.1.call-update) | async-done | bytes 4194320 | tf_op jit(solution)/shard_map/all_gather | solution.py:15
  150.1 0.0 copy-done.2
  150.1 4.1 %fusion.7 = bf16[256,512]{1,0:T(8,128)(2,1)S(1)} fusion(bf16[4096,512]{1,0:T(8,128)(2,1)} %all-gather.9.cloned.1.call-done, bf16[256,4096]{1,0:T(8,128)(2,1)} %all-gather.7.cloned.1.call-done, f32[4096]{0:T(1024)S(1)} %copy-done.2, f32[256]{0:T(256)S(1)} %add_rsqrt_fusion), kind=kOutput, calls=%fused_computation.12 | convolution fusion | flops 1078067200 | bytes 6571008 | tf_op jit(solution)/shard_map/dot_general | solution.py:20
  154.2 2.2 all_gather.18
  156.4 0.0 copy-done.1
  156.4 2.1 convolution_convert_fusion
  158.5 4.4 %all-to-all-start = ((bf16[8,128,1024]{2,1,0:T(8,128)(2,1)}), bf16[8,128,1024]{2,1,0:T(8,128)(2,1)}, u32[]{:S(2)}, u32[]{:S(2)}) async-start(bf16[8,128,1024]{2,1,0:T(8,128)(2,1)} %bitcast.8), calls=%async_computation | async-start | bytes 4194304 | tf_op jit(solution)/shard_map/all_to_all | solution.py:32
  162.9 69.8 %all-gather.11.cloned.1.call-done = bf16[1024,1024]{1,0:T(8,128)(2,1)} async-done(((bf16[1024,128]{1,0:T(8,128)(2,1)}), bf16[1024,1024]{1,0:T(8,128)(2,1)}) %all-gather.11.cloned.1.call-update) | async-done | bytes 2097168 | tf_op jit(solution)/shard_map/all_gather | solution.py:24
  232.7 3.1 %convolution_convert_fusion.2 = bf16[256,1024]{1,0:T(8,128)(2,1)} fusion(bf16[256,1024]{1,0:T(8,128)(2,1)S(1)} %all_gather.18, bf16[1024,1024]{1,0:T(8,128)(2,1)} %all-gather.11.cloned.1.call-done), kind=kOutput, calls=%fused_computation.11 | convolution fusion | flops 537133056 | bytes 3145728 | tf_op jit(solution)/shard_map/dot_general | solution.py:25
  235.8 0.0 all-to-all-done
  235.8 2.0 convert_reduce_fusion
  237.9 0.8 broadcast_multiply_fusion
  (1 shorter events, 0.0 us)
Async XLA Ops:
  7.2 55.0 %copy-start = (bf16[512,2048]{1,0:T(8,128)(2,1)S(1)}, bf16[512,2048]{1,0:T(8,128)(2,1)}, u32[]{:S(2)}) copy-start(bf16[512,2048]{1,0:T(8,128)(2,1)} %param.8) | copy-start | bytes 6291460
  7.2 55.0 %all-gather.5.cloned.1.call-start = ((), (), s32[]{:S(2)}) async-start(), calls=%async_computation.1 | async-start | bytes 2359296 | tf_op jit(solution)/shard_map/all_gather | solution.py:11
  7.9 64.9 %all-gather.7.cloned.1.call-start = ((), (), s32[]{:S(2)}) async-start(), calls=%async_computation.2 | async-start | bytes 3145728 | tf_op jit(solution)/shard_map/all_gather | solution.py:16
  8.7 141.4 %all-gather.9.cloned.1.call-start = ((), (), s32[]{:S(2)}) async-start(), calls=%async_computation.3 | async-start | bytes 4718592 | tf_op jit(solution)/shard_map/all_gather | solution.py:15
  65.8 84.3 %copy-start.2 = (f32[4096]{0:T(1024)S(1)}, f32[4096]{0:T(1024)}, u32[]{:S(2)}) copy-start(f32[4096]{0:T(1024)} %param.7) | copy-start | bytes 49156
  65.8 166.9 %all-gather.11.cloned.1.call-start = ((), (), s32[]{:S(2)}) async-start(), calls=%async_computation.4 | async-start | bytes 2359296 | tf_op jit(solution)/shard_map/all_gather | solution.py:24
  74.9 81.5 %copy-start.1 = (bf16[256,1024]{1,0:T(8,128)(2,1)S(1)}, bf16[256,1024]{1,0:T(8,128)(2,1)}, u32[]{:S(2)}) copy-start(bf16[256,1024]{1,0:T(8,128)(2,1)} %param.11) | copy-start | bytes 1572868
  158.5 77.3 %all-to-all-start = ((bf16[8,128,1024]{2,1,0:T(8,128)(2,1)}), bf16[8,128,1024]{2,1,0:T(8,128)(2,1)}, u32[]{:S(2)}, u32[]{:S(2)}) async-start(bf16[8,128,1024]{2,1,0:T(8,128)(2,1)} %bitcast.8), calls=%async_computation | async-start | bytes 4194304 | tf_op jit(solution)/shard_map/all_to_all | solution.py:32
Sparse Core Ops, SparseCore 0:
  10.1 51.9 all-gather.4
  63.7 9.0 all-gather.6
  75.5 74.5 all-gather.8
  152.0 80.6 all-gather.10

commit v2 on v1

v2 whole, which is shorter than its diff:
```python
import functools
import math

import jax
import jax.numpy as jnp
from jax import lax
from jax.experimental import pallas as pl
from jax.experimental.pallas import tpu as pltpu
from jax.sharding import PartitionSpec as P

MESH = pl.DeviceIdType.MESH
BF16, F32 = jnp.bfloat16, jnp.float32


class Gather:
    def __init__(self, place, buf, sems):
        self.place, self.buf = place, buf
        self.rin, self.ryn, self.sup, self.sdn, self.sx, self.sy = sems
        n, rows, _ = buf.shape
        self.n, self.split = n, rows % 128 == 0
        y = place["y"]
        if self.split:
            self.own_rows = pl.ds(pl.multiple_of(y * (3 * rows // 8), 16), 5 * rows // 8)
            self.y_out = pl.ds(pl.multiple_of(y * (5 * rows // 8), 16), 3 * rows // 8)
            self.y_in = pl.ds(pl.multiple_of((1 - y) * (5 * rows // 8), 16), 3 * rows // 8)
        else:
            self.own_rows = pl.ds(0, rows)

    def copy(self, slot, rows, send, recv, device):
        ref = self.buf.at[slot, rows, :]
        return pltpu.make_async_remote_copy(
            src_ref=ref, dst_ref=ref, send_sem=send, recv_sem=recv,
            device_id=device, device_id_type=MESH,
        )

    def up(self, k):
        p, slot = self.place, k * 2 + self.place["x"]
        return self.copy(slot, self.own_rows, self.sup.at[k], self.rin.at[slot], p["dev"](p["z"] + 1, p["x"]))

    def down(self, k):
        p, slot = self.place, k * 2 + self.place["x"]
        return self.copy(slot, self.own_rows, self.sdn.at[k], self.rin.at[slot], p["dev"](p["z"] - 1, p["x"]))

    def across(self, k):
        p, slot = self.place, k * 2 + self.place["x"]
        return self.copy(slot, self.own_rows, self.sx.at[k], self.rin.at[slot], p["dev"](p["z"], 1 - p["x"]))

    def plane(self, slot, rows):
        p = self.place
        return self.copy(slot, rows, self.sy.at[slot], self.ryn.at[slot], (1 - p["y"], p["g"], p["c"]))

    def arrived(self, slot):
        p = self.place
        self.copy(slot, self.own_rows, self.sx.at[0], self.rin.at[slot], p["dev"](p["z"], 1 - p["x"])).wait_recv()
        if self.split:
            self.plane(slot, self.y_out).start()

    def start(self):
        p = self.place
        z, nz = p["z"], p["nz"]

        @pl.when(z < nz - 1)
        def _():
            self.up(z).start()

        @pl.when(z > 0)
        def _():
            self.down(z).start()

        self.across(z).start()

    def run(self):
        p = self.place
        z, nz, x = p["z"], p["nz"], p["x"]

        def step(s, carry):
            @pl.when(jnp.logical_and(s < nz, z - s >= 0))
            def _():
                self.copy((z - s) * 2 + x, self.own_rows, self.sx.at[0], self.rin.at[(z - s) * 2 + x], p["dev"](z, 1 - x)).wait_recv()

                @pl.when(z < nz - 1)
                def _():
                    self.up(z - s).start()

                self.across(z - s).start()
                if self.split:
                    self.plane((z - s) * 2 + x, self.y_out).start()

            @pl.when(z + s < nz)
            def _():
                self.copy((z + s) * 2 + x, self.own_rows, self.sx.at[0], self.rin.at[(z + s) * 2 + x], p["dev"](z, 1 - x)).wait_recv()

                @pl.when(z > 0)
                def _():
                    self.down(z + s).start()

                self.across(z + s).start()
                if self.split:
                    self.plane((z + s) * 2 + x, self.y_out).start()

            @pl.when(z - (s - 1) >= 0)
            def _():
                self.arrived((z - (s - 1)) * 2 + 1 - x)

            @pl.when(jnp.logical_and(s > 1, z + (s - 1) < nz))
            def _():
                self.arrived((z + (s - 1)) * 2 + 1 - x)

            return carry

        lax.fori_loop(1, nz + 1, step, 0)
        if self.split:
            def take(slot, carry):
                @pl.when(slot != p["g"])
                def _():
                    self.plane(slot, self.y_in).wait_recv()
                return carry

            lax.fori_loop(0, self.n, take, 0)

    def drain(self):
        p = self.place
        z, nz = p["z"], p["nz"]

        def step(k, carry):
            @pl.when(jnp.logical_and(k <= z, z < nz - 1))
            def _():
                self.up(k).wait_send()

            @pl.when(jnp.logical_and(k >= z, z > 0))
            def _():
                self.down(k).wait_send()

            self.across(k).wait_send()
            return carry

        lax.fori_loop(0, nz, step, 0)
        if self.split:
            def sent(slot, carry):
                @pl.when(slot != p["g"])
                def _():
                    self.plane(slot, self.y_out).wait_send()
                return carry

            lax.fori_loop(0, self.n, sent, 0)


def kernel(n, inside, scale, *refs):
    it = iter(refs)
    tok_in, gain, width_in, old_in, head_in, cot_in = (next(it) for _ in range(6))
    grown_out = next(it)
    if inside:
        value_out, grad_out = next(it), next(it)
    else:
        mixed_out = next(it)
    tok, width, normed, mixed, oldb, grownb = (next(it) for _ in range(6))
    old_sems = [next(it) for _ in range(6)]
    grown_sems = [next(it) for _ in range(6)]
    local, pair_s, pair_r = next(it), next(it), next(it)
    if inside:
        headb, cot, tx, rx, tz, rz, own = (next(it) for _ in range(7))
        head_sems = [next(it) for _ in range(6)]
        xs, xr, zs, zr = (next(it) for _ in range(4))

    y, g, c = lax.axis_index("trial"), lax.axis_index("fsdp"), lax.axis_index("tensor")
    nz = n // 2
    z, x = g // 2, g % 2

    def dev(zz, xx):
        return (y, zz * 2 + xx, c)

    place = dict(y=y, g=g, c=c, z=z, x=x, nz=nz, dev=dev)

    loads = [
        pltpu.make_async_copy(old_in, oldb.at[g], local.at[0]),
        pltpu.make_async_copy(tok_in, tok.at[c], local.at[1]),
        pltpu.make_async_copy(width_in, width, local.at[2]),
    ]
    if inside:
        loads.append(pltpu.make_async_copy(head_in, headb.at[g], local.at[3]))
        loads.append(pltpu.make_async_copy(cot_in, cot, local.at[4]))
    for load in loads:
        load.start()

    barrier = pltpu.get_barrier_semaphore()

    def greet(k, carry):
        @pl.when(k != z)
        def _():
            pl.semaphore_signal(barrier, inc=1, device_id=dev(k, x), device_id_type=MESH)
        return carry

    lax.fori_loop(0, nz, greet, 0)
    core = (y, g, 1 - c)
    for other in (dev(z, 1 - x), (1 - y, g, c), core):
        pl.semaphore_signal(barrier, inc=1, device_id=other, device_id_type=MESH)
    pl.semaphore_wait(barrier, nz - 1 + 3)

    old = Gather(place, oldb, old_sems)
    grown = Gather(place, grownb, grown_sems)
    loads[0].wait()
    old.start()
    loads[1].wait()
    swap = pltpu.make_async_remote_copy(
        src_ref=tok.at[c], dst_ref=tok.at[c], send_sem=pair_s.at[0], recv_sem=pair_r.at[0],
        device_id=core, device_id_type=MESH,
    )
    swap.start()
    swap.wait()

    count, half_d = tok.shape[1], tok.shape[2]

    @pl.loop(0, count // 16)
    def _(i):
        rows = pl.ds(pl.multiple_of(i * 16, 16), 16)
        a, b = tok[0, rows, :].astype(F32), tok[1, rows, :].astype(F32)
        total = jnp.sum(a * a, axis=-1, keepdims=True) + jnp.sum(b * b, axis=-1, keepdims=True)
        inv = lax.rsqrt(total * (1.0 / (2 * half_d)) + 1e-05)
        normed[rows, pl.ds(0, half_d)] = (a * inv * gain[:, pl.ds(0, half_d)]).astype(BF16)
        normed[rows, pl.ds(half_d, half_d)] = (b * inv * gain[:, pl.ds(half_d, half_d)]).astype(BF16)

    old.run()
    if inside:
        head = Gather(place, headb, head_sems)
        loads[3].wait()
        head.start()
    loads[2].wait()
    feats = oldb.shape[2]

    @pl.loop(0, feats // 256)
    def _(j):
        cols = pl.ds(pl.multiple_of(j * 256, 256), 256)
        rhs = oldb[:, :, cols].reshape(-1, 256)
        grownb[g, :, cols] = jnp.dot(width[...], rhs, preferred_element_type=F32).astype(BF16)

    grown.start()
    grown_out[...] = grownb[g]
    grown.run()

    @pl.loop(0, feats // 256)
    def _(j):
        cols = pl.ds(pl.multiple_of(j * 256, 256), 256)
        rhs = grownb[:, :, cols].reshape(-1, 256)
        mixed[c, :, cols] = jnp.dot(normed[...], rhs, preferred_element_type=F32).astype(BF16)

    share = pltpu.make_async_remote_copy(
        src_ref=mixed.at[c], dst_ref=mixed.at[c], send_sem=pair_s.at[1], recv_sem=pair_r.at[1],
        device_id=core, device_id_type=MESH,
    )
    share.start()
    share.wait()

    if inside:
        w = headb.shape[2]
        per_half = n // 2
        loads[4].wait()

        def block(slot):
            cols = pl.ds(pl.multiple_of((slot % per_half) * w, w), w)
            return mixed[slot // per_half, :, cols]

        def partial(slot):
            return lax.dot_general(
                block(slot), cot[...], (((0,), (0,)), ((), ())), preferred_element_type=F32
            )

        def hop(k):
            return pltpu.make_async_remote_copy(
                src_ref=tx.at[k], dst_ref=rx.at[k], send_sem=xs.at[k], recv_sem=xr.at[k],
                device_id=dev(z, 1 - x), device_id_type=MESH,
            )

        def deliver(k):
            return pltpu.make_async_remote_copy(
                src_ref=tz.at[k], dst_ref=rz.at[z], send_sem=zs.at[k], recv_sem=zr.at[z],
                device_id=dev(k, x), device_id_type=MESH,
            )

        def receive(k):
            return pltpu.make_async_remote_copy(
                src_ref=tz.at[k], dst_ref=rz.at[k], send_sem=zs.at[k], recv_sem=zr.at[k],
                device_id=dev(k, x), device_id_type=MESH,
            )

        def first(i, carry):
            k = (z + 1 + i) % nz
            tx[k] = partial(k * 2 + 1 - x).astype(BF16)
            hop(k).start()
            return carry

        lax.fori_loop(0, nz, first, 0)
        head.run()

        def second(i, carry):
            k = (z + 1 + i) % nz
            mine = partial(k * 2 + x)
            hop(k).wait_recv()
            mine = mine + rx[k].astype(F32)

            @pl.when(k != z)
            def _():
                tz[k] = mine.astype(BF16)
                deliver(k).start()

            @pl.when(k == z)
            def _():
                own[...] = mine
            return carry

        lax.fori_loop(0, nz, second, 0)

        @pl.loop(0, value_out.shape[1] // 256)
        def _(j):
            outs = pl.ds(pl.multiple_of(j * 256, 256), 256)
            total = jnp.zeros((count, 256), F32)
            for slot in range(n):
                lhs = mixed[slot // per_half, :, pl.ds((slot % per_half) * w, w)]
                total = total + lax.dot_general(
                    lhs, headb[slot, outs, :], (((1,), (1,)), ((), ())), preferred_element_type=F32
                )
            value_out[:, outs] = total.astype(BF16)

        def collect(k, carry):
            @pl.when(k != z)
            def _():
                receive(k).wait_recv()
                own[...] += rz[k].astype(F32)
            return carry

        lax.fori_loop(0, nz, collect, 0)
        grad_out[...] = own[...] * scale

        def sent(k, carry):
            hop(k).wait_send()

            @pl.when(k != z)
            def _():
                deliver(k).wait_send()
            return carry

        lax.fori_loop(0, nz, sent, 0)
        head.drain()
    else:
        mixed_out[...] = mixed[...]
    old.drain()
    grown.drain()


def gather_sems(n):
    dma = pltpu.SemaphoreType.DMA
    return [dma((n,)), dma((n,)), dma((n // 2,)), dma((n // 2,)), dma((n // 2,)), dma((n,))]


def per_device(tokens, norm_gain, grow_width, old_value, grow_head, cotangent):
    n = lax.axis_size("fsdp")
    count, half_d = tokens.shape
    feats = old_value.shape[1]
    slab = grow_width.shape[0]
    heads, w = grow_head.shape
    inside = w % 128 == 0
    scale = 1.0 / math.sqrt(count * n)
    dma = pltpu.SemaphoreType.DMA
    vm = pl.BlockSpec(memory_space=pltpu.VMEM)
    hbm = pl.BlockSpec(memory_space=pl.ANY)
    outs = [jax.ShapeDtypeStruct((slab, feats), BF16)]
    if inside:
        outs += [jax.ShapeDtypeStruct((count, heads), BF16), jax.ShapeDtypeStruct((w, heads), F32)]
    else:
        outs += [jax.ShapeDtypeStruct((2, count, feats), BF16)]
    scratch = [
        pltpu.VMEM((2, count, half_d), BF16),
        pltpu.VMEM(grow_width.shape, BF16),
        pltpu.VMEM((count, 2 * half_d), BF16),
        pltpu.VMEM((2, count, feats), BF16),
        pltpu.VMEM((n,) + old_value.shape, BF16),
        pltpu.VMEM((n, slab, feats), BF16),
        *gather_sems(n), *gather_sems(n),
        dma((5,)), dma((2,)), dma((2,)),
    ]
    if inside:
        piece = pltpu.VMEM((n // 2, w, heads), BF16)
        scratch += [
            pltpu.VMEM((n, heads, w), BF16), pltpu.VMEM((count, heads), BF16),
            piece, piece, piece, piece, pltpu.VMEM((w, heads), F32),
            *gather_sems(n),
            dma((n // 2,)), dma((n // 2,)), dma((n // 2,)), dma((n // 2,)),
        ]
    results = pl.pallas_call(
        functools.partial(kernel, n, inside, scale),
        out_shape=outs,
        in_specs=[hbm, vm, hbm, hbm, hbm, hbm],
        out_specs=[vm] * len(outs),
        scratch_shapes=scratch,
        compiler_params=pltpu.CompilerParams(
            collective_id=0, has_side_effects=True, vmem_limit_bytes=48 * 1024 * 1024
        ),
    )(tokens, norm_gain.reshape(1, -1), grow_width, old_value, grow_head, cotangent)
    if inside:
        return tuple(results)
    grown_value, halves = results
    mixed = jnp.concatenate([halves[0], halves[1]], axis=1)
    head_all = lax.all_gather(grow_head, "fsdp", axis=1, tiled=True)
    value_out = lax.dot_general(
        mixed, head_all, (((1,), (1,)), ((), ())), preferred_element_type=F32
    ).astype(BF16)
    partial = lax.dot_general(
        mixed, cotangent, (((0,), (0,)), ((), ())), preferred_element_type=F32
    ).astype(BF16)
    partial = partial.reshape(n, partial.shape[0] // n, partial.shape[1])
    parts = lax.all_to_all(partial, "fsdp", split_axis=0, concat_axis=0, tiled=True)
    return (grown_value, value_out, jnp.sum(parts.astype(F32), axis=0) * scale)


def solution(mesh):
    return jax.shard_map(
        per_device,
        mesh=mesh,
        in_specs=(
            P(("trial", "fsdp"), "tensor"),
            P(),
            P("fsdp", None),
            P("fsdp", "tensor"),
            P("tensor", "fsdp"),
            P(("trial", "fsdp"), "tensor"),
        ),
        out_specs=(
            P(("trial", "fsdp"), "tensor"),
            P(("trial", "fsdp"), "tensor"),
            P(("trial", "fsdp"), "tensor"),
        ),
        check_vma=False,
    )
```

time: 246 us -> 144 us (0.59)
  the two profiles are of different devices: /device:TPU:0 before, /device:TPU:9 now
where the time goes in v2:
time: 144 us
  Pallas kernels  134 us (93%)
  local copies, waits for them, and re-layouts  8.85 us (6%)
    pallas_call x1, Pallas kernels, per_device(): pl.pallas_call(functools.partial(kernel, n, inside, scale), out_shape=out...  134 us
    unnamed x15, local copies, waits for them, and re-layouts  8.85 us

profile of v2, /device:TPU:9, one launch (start us, length us, event | category | flops | bytes accessed | tf_op | source)
XLA Modules:
  0.0 143.6 jit_solution(8790031670174903481)
XLA Ops:
  0.6 0.0 copy-start
  0.6 1.6 %copy-done = bf16[512,2048]{1,0:T(8,128)(2,1)S(1)} copy-done((bf16[512,2048]{1,0:T(8,128)(2,1)S(1)}, bf16[512,2048]{1,0:T(8,128)(2,1)}, u32[]{:S(2)}) %copy-start) | copy-done | bytes 2097176
  2.2 0.0 copy-start.1
  2.2 1.2 copy-done.1
  3.4 0.0 copy-start.2
  3.5 1.0 copy-done.2
  4.5 0.0 copy-start.3
  4.5 0.9 copy-done.3
  5.4 0.0 copy-start.4
  5.4 0.9 copy-done.4
  6.4 0.0 copy-start.5
  6.4 0.7 copy-done.5
  7.1 134.1 %shard_map.85 = (bf16[512,512]{1,0:T(8,128)(2,1)S(1)}, bf16[256,1024]{1,0:T(8,128)(2,1)S(1)}, f32[128,1024]{1,0:T(8,128)S(1)}) custom-call(bf16[256,2048]{1,0:T(8,128)(2,1)S(1)} %copy-done.1, f32[1,4096]{1,0:T(1,128)S(1)} %bitcast.1, bf16[512,2048]{1,0:T(8,128)(2,1)S(1)} %copy-done, bf16[256,512]{1,0:T(8,128)(2,1)S(1)} %copy-done.3, ...), custom_call_target="tpu_custom_call" | custom-call | tf_op jit(solution)/shard_map/pallas_call | solution.py:388
  141.2 0.8 copy.12
  142.0 0.8 copy.13
  142.8 0.8 copy.14
Async XLA Ops:
  0.6 1.6 %copy-start = (bf16[512,2048]{1,0:T(8,128)(2,1)S(1)}, bf16[512,2048]{1,0:T(8,128)(2,1)}, u32[]{:S(2)}) copy-start(bf16[512,2048]{1,0:T(8,128)(2,1)} %refs_2_.1) | copy-start | bytes 6291460
  2.2 1.2 copy-start.1
  3.4 1.0 copy-start.2
  4.5 0.9 copy-start.3
  5.4 0.9 copy-start.4
  6.4 0.7 copy-start.5

commit v3 on v2

--- a/solution.py
+++ b/solution.py
@@ -69,46 +69,43 @@
 
         self.across(z).start()
 
-    def run(self):
+    def step(self, s):
         p = self.place
         z, nz, x = p["z"], p["nz"], p["x"]
-
-        def step(s, carry):
-            @pl.when(jnp.logical_and(s < nz, z - s >= 0))
-            def _():
-                self.copy((z - s) * 2 + x, self.own_rows, self.sx.at[0], self.rin.at[(z - s) * 2 + x], p["dev"](z, 1 - x)).wait_recv()
-
-                @pl.when(z < nz - 1)
-                def _():
-                    self.up(z - s).start()
-
-                self.across(z - s).start()
-                if self.split:
-                    self.plane((z - s) * 2 + x, self.y_out).start()
-
-            @pl.when(z + s < nz)
-            def _():
-                self.copy((z + s) * 2 + x, self.own_rows, self.sx.at[0], self.rin.at[(z + s) * 2 + x], p["dev"](z, 1 - x)).wait_recv()
-
-                @pl.when(z > 0)
-                def _():
-                    self.down(z + s).start()
-
-                self.across(z + s).start()
-                if self.split:
-                    self.plane((z + s) * 2 + x, self.y_out).start()
-
-            @pl.when(z - (s - 1) >= 0)
-            def _():
-                self.arrived((z - (s - 1)) * 2 + 1 - x)
-
-            @pl.when(jnp.logical_and(s > 1, z + (s - 1) < nz))
-            def _():
-                self.arrived((z + (s - 1)) * 2 + 1 - x)
-
-            return carry
-
-        lax.fori_loop(1, nz + 1, step, 0)
+        @pl.when(jnp.logical_and(s < nz, z - s >= 0))
+        def _():
+            self.copy((z - s) * 2 + x, self.own_rows, self.sx.at[0], self.rin.at[(z - s) * 2 + x], p["dev"](z, 1 - x)).wait_recv()
+
+            @pl.when(z < nz - 1)
+            def _():
+                self.up(z - s).start()
+
+            self.across(z - s).start()
+            if self.split:
+                self.plane((z - s) * 2 + x, self.y_out).start()
+
+        @pl.when(z + s < nz)
+        def _():
+            self.copy((z + s) * 2 + x, self.own_rows, self.sx.at[0], self.rin.at[(z + s) * 2 + x], p["dev"](z, 1 - x)).wait_recv()
+
+            @pl.when(z > 0)
+            def _():
+                self.down(z + s).start()
+
+            self.across(z + s).start()
+            if self.split:
+                self.plane((z + s) * 2 + x, self.y_out).start()
+
+        @pl.when(z - (s - 1) >= 0)
+        def _():
+            self.arrived((z - (s - 1)) * 2 + 1 - x)
+
+        @pl.when(jnp.logical_and(s > 1, z + (s - 1) < nz))
+        def _():
+            self.arrived((z + (s - 1)) * 2 + 1 - x)
+
+    def finish(self):
+        p = self.place
         if self.split:
             def take(slot, carry):
                 @pl.when(slot != p["g"])
@@ -158,9 +155,9 @@
     grown_sems = [next(it) for _ in range(6)]
     local, pair_s, pair_r = next(it), next(it), next(it)
     if inside:
-        headb, cot, tx, rx, tz, rz, own = (next(it) for _ in range(7))
+        headb, cot, theirs, tz, ru, rd, own = (next(it) for _ in range(7))
         head_sems = [next(it) for _ in range(6)]
-        xs, xr, zs, zr = (next(it) for _ in range(4))
+        xs, xr, zs, ur, dr = (next(it) for _ in range(5))
 
     y, g, c = lax.axis_index("trial"), lax.axis_index("fsdp"), lax.axis_index("tensor")
     nz = n // 2
@@ -178,7 +175,7 @@
     ]
     if inside:
         loads.append(pltpu.make_async_copy(head_in, headb.at[g], local.at[3]))
-        loads.append(pltpu.make_async_copy(cot_in, cot, local.at[4]))
+        loads.append(pltpu.make_async_copy(cot_in, cot.at[0], local.at[4]))
     for load in loads:
         load.start()
 
@@ -206,9 +203,36 @@
         device_id=core, device_id_type=MESH,
     )
     swap.start()
+    count, half_d = tok.shape[1], tok.shape[2]
+
+    def walk_old(s, carry):
+        old.step(s)
+        return carry
+
+    lax.fori_loop(1, nz + 1, walk_old, 0)
+    old.finish()
+    if inside:
+        head = Gather(place, headb, head_sems)
+        loads[3].wait()
+        head.start()
+        loads[4].wait()
+        lend = pltpu.make_async_remote_copy(
+            src_ref=cot.at[0], dst_ref=cot.at[1], send_sem=pair_s.at[2], recv_sem=pair_r.at[2],
+            device_id=dev(z, 1 - x), device_id_type=MESH,
+        )
+        lend.start()
+    loads[2].wait()
+    feats = oldb.shape[2]
+
+    @pl.loop(0, feats // 256)
+    def _(j):
+        cols = pl.ds(pl.multiple_of(j * 256, 256), 256)
+        rhs = oldb[:, :, cols].reshape(-1, 256)
+        grownb[g, :, cols] = jnp.dot(width[...], rhs, preferred_element_type=F32).astype(BF16)
+
+    grown.start()
+    grown_out[...] = grownb[g]
     swap.wait()
-
-    count, half_d = tok.shape[1], tok.shape[2]
 
     @pl.loop(0, count // 16)
     def _(i):
@@ -219,23 +243,14 @@
         normed[rows, pl.ds(0, half_d)] = (a * inv * gain[:, pl.ds(0, half_d)]).astype(BF16)
         normed[rows, pl.ds(half_d, half_d)] = (b * inv * gain[:, pl.ds(half_d, half_d)]).astype(BF16)
 
-    old.run()
-    if inside:
-        head = Gather(place, headb, head_sems)
-        loads[3].wait()
-        head.start()
-    loads[2].wait()
-    feats = oldb.shape[2]
-
-    @pl.loop(0, feats // 256)
-    def _(j):
-        cols = pl.ds(pl.multiple_of(j * 256, 256), 256)
-        rhs = oldb[:, :, cols].reshape(-1, 256)
-        grownb[g, :, cols] = jnp.dot(width[...], rhs, preferred_element_type=F32).astype(BF16)
-
-    grown.start()
-    grown_out[...] = grownb[g]
-    grown.run()
+    def walk_grown(s, carry):
+        if inside:
+            head.step(s)
+        grown.step(s)
+        return carry
+
+    lax.fori_loop(1, nz + 1, walk_grown, 0)
+    grown.finish()
 
     @pl.loop(0, feats // 256)
     def _(j):
@@ -253,61 +268,84 @@
     if inside:
         w = headb.shape[2]
         per_half = n // 2
-        loads[4].wait()
 
         def block(slot):
             cols = pl.ds(pl.multiple_of((slot % per_half) * w, w), w)
-            return mixed[slot // per_half, :, cols]
-
-        def partial(slot):
-            return lax.dot_general(
-                block(slot), cot[...], (((0,), (0,)), ((), ())), preferred_element_type=F32
+            return mixed.at[slot // per_half, :, cols]
+
+        def hand(k):
+            return pltpu.make_async_remote_copy(
+                src_ref=block(k * 2 + 1 - x), dst_ref=theirs.at[k], send_sem=xs.at[k],
+                recv_sem=xr.at[k], device_id=dev(z, 1 - x), device_id_type=MESH,
             )
 
-        def hop(k):
+        def offer(i, carry):
+            @pl.when(nz - 1 - i > i)
+            def _():
+                hand(nz - 1 - i).start()
+
+            @pl.when(nz - 1 - i >= i)
+            def _():
+                hand(i).start()
+            return carry
+
+        lax.fori_loop(0, nz, offer, 0)
+        lend.wait_recv()
+
+        def partial(k):
+            rows = (((0,), (0,)), ((), ()))
+            mine = lax.dot_general(block(k * 2 + x)[...], cot[0], rows, preferred_element_type=F32)
+            return mine + lax.dot_general(theirs[k], cot[1], rows, preferred_element_type=F32)
+
+        def rise(k):
             return pltpu.make_async_remote_copy(
-                src_ref=tx.at[k], dst_ref=rx.at[k], send_sem=xs.at[k], recv_sem=xr.at[k],
-                device_id=dev(z, 1 - x), device_id_type=MESH,
+                src_ref=tz.at[k], dst_ref=ru.at[k], send_sem=zs.at[k], recv_sem=ur.at[k],
+                device_id=dev(z + 1, x), device_id_type=MESH,
             )
 
-        def deliver(k):
+        def sink(k):
             return pltpu.make_async_remote_copy(
-                src_ref=tz.at[k], dst_ref=rz.at[z], send_sem=zs.at[k], recv_sem=zr.at[z],
-                device_id=dev(k, x), device_id_type=MESH,
+                src_ref=tz.at[k], dst_ref=rd.at[k], send_sem=zs.at[k], recv_sem=dr.at[k],
+                device_id=dev(z - 1, x), device_id_type=MESH,
             )
 
-        def receive(k):
-            return pltpu.make_async_remote_copy(
-                src_ref=tz.at[k], dst_ref=rz.at[k], send_sem=zs.at[k], recv_sem=zr.at[k],
-                device_id=dev(k, x), device_id_type=MESH,
-            )
-
-        def first(i, carry):
-            k = (z + 1 + i) % nz
-            tx[k] = partial(k * 2 + 1 - x).astype(BF16)
-            hop(k).start()
+        def mine(k, carry):
+            hand(k).wait_recv()
             return carry
 
-        lax.fori_loop(0, nz, first, 0)
-        head.run()
-
-        def second(i, carry):
-            k = (z + 1 + i) % nz
-            mine = partial(k * 2 + x)
-            hop(k).wait_recv()
-            mine = mine + rx[k].astype(F32)
-
-            @pl.when(k != z)
-            def _():
-                tz[k] = mine.astype(BF16)
-                deliver(k).start()
-
-            @pl.when(k == z)
-            def _():
-                own[...] = mine
+        lax.fori_loop(0, nz, mine, 0)
+
+        def chain(i, carry):
+            k = nz - 1 - i
+
+            @pl.when(k > z)
+            def _():
+                own[...] = partial(k)
+
+                @pl.when(z > 0)
+                def _():
+                    rise(k).wait_recv()
+                    own[...] += ru[k].astype(F32)
+
+                tz[k] = own[...].astype(BF16)
+                rise(k).start()
+
+            @pl.when(i < z)
+            def _():
+                own[...] = partial(i)
+
+                @pl.when(z < nz - 1)
+                def _():
+                    sink(i).wait_recv()
+                    own[...] += rd[i].astype(F32)
+
+                tz[i] = own[...].astype(BF16)
+                sink(i).start()
             return carry
 
-        lax.fori_loop(0, nz, second, 0)
+        lax.fori_loop(0, nz - 1, chain, 0)
+        own[...] = partial(z)
+        head.finish()
 
         @pl.loop(0, value_out.shape[1] // 256)
         def _(j):
@@ -320,22 +358,29 @@
                 )
             value_out[:, outs] = total.astype(BF16)
 
-        def collect(k, carry):
-            @pl.when(k != z)
-            def _():
-                receive(k).wait_recv()
-                own[...] += rz[k].astype(F32)
-            return carry
-
-        lax.fori_loop(0, nz, collect, 0)
+        @pl.when(z > 0)
+        def _():
+            rise(z).wait_recv()
+            own[...] += ru[z].astype(F32)
+
+        @pl.when(z < nz - 1)
+        def _():
+            sink(z).wait_recv()
+            own[...] += rd[z].astype(F32)
+
         grad_out[...] = own[...] * scale
+        lend.wait_send()
 
         def sent(k, carry):
-            hop(k).wait_send()
-
-            @pl.when(k != z)
-            def _():
-                deliver(k).wait_send()
+            hand(k).wait_send()
+
+            @pl.when(k > z)
+            def _():
+                rise(k).wait_send()
+
+            @pl.when(k < z)
+            def _():
+                sink(k).wait_send()
             return carry
 
         lax.fori_loop(0, nz, sent, 0)
@@ -375,15 +420,15 @@
         pltpu.VMEM((n,) + old_value.shape, BF16),
         pltpu.VMEM((n, slab, feats), BF16),
         *gather_sems(n), *gather_sems(n),
-        dma((5,)), dma((2,)), dma((2,)),
+        dma((5,)), dma((3,)), dma((3,)),
     ]
     if inside:
         piece = pltpu.VMEM((n // 2, w, heads), BF16)
         scratch += [
-            pltpu.VMEM((n, heads, w), BF16), pltpu.VMEM((count, heads), BF16),
-            piece, piece, piece, piece, pltpu.VMEM((w, heads), F32),
+            pltpu.VMEM((n, heads, w), BF16), pltpu.VMEM((2, count, heads), BF16),
+            pltpu.VMEM((n // 2, count, w), BF16), piece, piece, piece, pltpu.VMEM((w, heads), F32),
             *gather_sems(n),
-            dma((n // 2,)), dma((n // 2,)), dma((n // 2,)), dma((n // 2,)),
+            dma((n // 2,)), dma((n // 2,)), dma((n // 2,)), dma((n // 2,)), dma((n // 2,)),
         ]
     results = pl.pallas_call(
         functools.partial(kernel, n, inside, scale),

time: 144 us -> 135 us (0.938)
  the two profiles are of different devices: /device:TPU:9 before, /device:TPU:0 now
where the time goes in v3:
time: 135 us
  Pallas kernels  125 us (93%)
  local copies, waits for them, and re-layouts  8.85 us (7%)
    pallas_call x1, Pallas kernels, per_device(): pl.pallas_call(functools.partial(kernel, n, inside, scale), out_shape=out...  125 us
    unnamed x15, local copies, waits for them, and re-layouts  8.85 us

profile of v3, /device:TPU:0, one launch (start us, length us, event | category | flops | bytes accessed | tf_op | source)
XLA Modules:
  0.0 134.8 jit_solution(1201071399208991368)
XLA Ops:
  0.6 0.0 copy-start
  0.6 1.6 %copy-done = bf16[512,2048]{1,0:T(8,128)(2,1)S(1)} copy-done((bf16[512,2048]{1,0:T(8,128)(2,1)S(1)}, bf16[512,2048]{1,0:T(8,128)(2,1)}, u32[]{:S(2)}) %copy-start) | copy-done | bytes 2097176
  2.2 0.0 copy-start.1
  2.2 1.2 copy-done.1
  3.4 0.0 copy-start.2
  3.5 1.0 copy-done.2
  4.5 0.0 copy-start.3
  4.5 0.9 copy-done.3
  5.4 0.0 copy-start.4
  5.4 0.9 copy-done.4
  6.4 0.0 copy-start.5
  6.4 0.7 copy-done.5
  7.1 125.3 %shard_map.85 = (bf16[512,512]{1,0:T(8,128)(2,1)S(1)}, bf16[256,1024]{1,0:T(8,128)(2,1)S(1)}, f32[128,1024]{1,0:T(8,128)S(1)}) custom-call(bf16[256,2048]{1,0:T(8,128)(2,1)S(1)} %copy-done.1, f32[1,4096]{1,0:T(1,128)S(1)} %bitcast.1, bf16[512,2048]{1,0:T(8,128)(2,1)S(1)} %copy-done, bf16[256,512]{1,0:T(8,128)(2,1)S(1)} %copy-done.3, ...), custom_call_target="tpu_custom_call" | custom-call | tf_op jit(solution)/shard_map/pallas_call | solution.py:433
  132.4 0.8 copy.12
  133.2 0.8 copy.13
  134.0 0.8 copy.14
Async XLA Ops:
  0.6 1.6 %copy-start = (bf16[512,2048]{1,0:T(8,128)(2,1)S(1)}, bf16[512,2048]{1,0:T(8,128)(2,1)}, u32[]{:S(2)}) copy-start(bf16[512,2048]{1,0:T(8,128)(2,1)} %refs_2_.1) | copy-start | bytes 6291460
  2.2 1.2 copy-start.1
  3.4 1.0 copy-start.2
  4.5 0.9 copy-start.3
  5.4 0.9 copy-start.4
  6.4 0.7 copy-start.5

commit v4 on v3

--- a/solution.py
+++ b/solution.py
@@ -13,18 +13,19 @@
 
 
 class Gather:
-    def __init__(self, place, buf, sems):
+    def __init__(self, place, buf, sems, part=0, parts=1):
         self.place, self.buf = place, buf
         self.rin, self.ryn, self.sup, self.sdn, self.sx, self.sy = sems
-        n, rows, _ = buf.shape
+        n, rows = buf.shape[0], buf.shape[1] // parts
+        base = part * rows
         self.n, self.split = n, rows % 128 == 0
         y = place["y"]
         if self.split:
-            self.own_rows = pl.ds(pl.multiple_of(y * (3 * rows // 8), 16), 5 * rows // 8)
-            self.y_out = pl.ds(pl.multiple_of(y * (5 * rows // 8), 16), 3 * rows // 8)
-            self.y_in = pl.ds(pl.multiple_of((1 - y) * (5 * rows // 8), 16), 3 * rows // 8)
+            self.own_rows = pl.ds(pl.multiple_of(base + y * (3 * rows // 8), 16), 5 * rows // 8)
+            self.y_out = pl.ds(pl.multiple_of(base + y * (5 * rows // 8), 16), 3 * rows // 8)
+            self.y_in = pl.ds(pl.multiple_of(base + (1 - y) * (5 * rows // 8), 16), 3 * rows // 8)
         else:
-            self.own_rows = pl.ds(0, rows)
+            self.own_rows = pl.ds(base, rows)
 
     def copy(self, slot, rows, send, recv, device):
         ref = self.buf.at[slot, rows, :]
@@ -151,8 +152,9 @@
     else:
         mixed_out = next(it)
     tok, width, normed, mixed, oldb, grownb = (next(it) for _ in range(6))
-    old_sems = [next(it) for _ in range(6)]
-    grown_sems = [next(it) for _ in range(6)]
+    old_parts, grown_parts = cuts(oldb.shape[1]), cuts(grownb.shape[1])
+    old_sems = [[next(it) for _ in range(6)] for _ in range(old_parts)]
+    grown_sems = [[next(it) for _ in range(6)] for _ in range(grown_parts)]
     local, pair_s, pair_r = next(it), next(it), next(it)
     if inside:
         headb, cot, theirs, tz, ru, rd, own = (next(it) for _ in range(7))
@@ -193,10 +195,11 @@
         pl.semaphore_signal(barrier, inc=1, device_id=other, device_id_type=MESH)
     pl.semaphore_wait(barrier, nz - 1 + 3)
 
-    old = Gather(place, oldb, old_sems)
-    grown = Gather(place, grownb, grown_sems)
+    old = [Gather(place, oldb, sems, i, old_parts) for i, sems in enumerate(old_sems)]
+    grown = [Gather(place, grownb, sems, i, grown_parts) for i, sems in enumerate(grown_sems)]
     loads[0].wait()
-    old.start()
+    for part in old:
+        part.start()
     loads[1].wait()
     swap = pltpu.make_async_remote_copy(
         src_ref=tok.at[c], dst_ref=tok.at[c], send_sem=pair_s.at[0], recv_sem=pair_r.at[0],
@@ -205,32 +208,45 @@
     swap.start()
     count, half_d = tok.shape[1], tok.shape[2]
 
-    def walk_old(s, carry):
-        old.step(s)
-        return carry
-
-    lax.fori_loop(1, nz + 1, walk_old, 0)
-    old.finish()
     if inside:
         head = Gather(place, headb, head_sems)
         loads[3].wait()
         head.start()
+    if inside:
         loads[4].wait()
         lend = pltpu.make_async_remote_copy(
             src_ref=cot.at[0], dst_ref=cot.at[1], send_sem=pair_s.at[2], recv_sem=pair_r.at[2],
             device_id=dev(z, 1 - x), device_id_type=MESH,
         )
         lend.start()
+
+    def walk_old(s, carry):
+        for part in old:
+            part.step(s)
+        if inside:
+            head.step(s)
+        return carry
+
+    lax.fori_loop(1, nz + 1, walk_old, 0)
+    for part in old:
+        part.finish()
     loads[2].wait()
     feats = oldb.shape[2]
 
-    @pl.loop(0, feats // 256)
-    def _(j):
-        cols = pl.ds(pl.multiple_of(j * 256, 256), 256)
-        rhs = oldb[:, :, cols].reshape(-1, 256)
-        grownb[g, :, cols] = jnp.dot(width[...], rhs, preferred_element_type=F32).astype(BF16)
-
-    grown.start()
+    slab = width.shape[0] // grown_parts
+    for i, part in enumerate(grown):
+        rows = pl.ds(i * slab, slab)
+
+        @pl.loop(0, feats // 256)
+        def _(j):
+            cols = pl.ds(pl.multiple_of(j * 256, 256), 256)
+            rhs = oldb[:, :, cols].reshape(-1, 256)
+            grownb[g, rows, cols] = jnp.dot(
+                width[rows, :], rhs, preferred_element_type=F32
+            ).astype(BF16)
+
+        part.start()
+
     grown_out[...] = grownb[g]
     swap.wait()
 
@@ -244,13 +260,13 @@
         normed[rows, pl.ds(half_d, half_d)] = (b * inv * gain[:, pl.ds(half_d, half_d)]).astype(BF16)
 
     def walk_grown(s, carry):
-        if inside:
-            head.step(s)
-        grown.step(s)
+        for part in grown:
+            part.step(s)
         return carry
 
     lax.fori_loop(1, nz + 1, walk_grown, 0)
-    grown.finish()
+    for part in grown:
+        part.finish()
 
     @pl.loop(0, feats // 256)
     def _(j):
@@ -387,8 +403,12 @@
         head.drain()
     else:
         mixed_out[...] = mixed[...]
-    old.drain()
-    grown.drain()
+    for part in old + grown:
+        part.drain()
+
+
+def cuts(rows):
+    return 2 if rows % 256 == 0 else 1
 
 
 def gather_sems(n):
@@ -419,7 +439,7 @@
         pltpu.VMEM((2, count, feats), BF16),
         pltpu.VMEM((n,) + old_value.shape, BF16),
         pltpu.VMEM((n, slab, feats), BF16),
-        *gather_sems(n), *gather_sems(n),
+        *(gather_sems(n) * cuts(old_value.shape[0])), *(gather_sems(n) * cuts(slab)),
         dma((5,)), dma((3,)), dma((3,)),
     ]
     if inside:

time: 135 us -> 134 us (level)
    pallas_call x1, Pallas kernels: 125 us -> 124 us  [per_device(): pl.pallas_call(functools.partial(kernel, n, inside, scale), out_shape=out...]
where the time goes in v4:
time: 134 us; the launch traced here: 133 us
  Pallas kernels  124 us (93%)
  local copies, waits for them, and re-layouts  8.85 us (7%)
    pallas_call x1, Pallas kernels, per_device(): pl.pallas_call(functools.partial(kernel, n, inside, scale), out_shape=out...  124 us
    unnamed x15, local copies, waits for them, and re-layouts  8.85 us

profile of v4, /device:TPU:0, one launch (start us, length us, event | category | flops | bytes accessed | tf_op | source)
XLA Modules:
  0.0 133.3 jit_solution(8178773220434632001)
XLA Ops:
  0.6 0.0 copy-start
  0.6 1.6 %copy-done = bf16[512,2048]{1,0:T(8,128)(2,1)S(1)} copy-done((bf16[512,2048]{1,0:T(8,128)(2,1)S(1)}, bf16[512,2048]{1,0:T(8,128)(2,1)}, u32[]{:S(2)}) %copy-start) | copy-done | bytes 2097176
  2.2 0.0 copy-start.1
  2.2 1.2 copy-done.1
  3.4 0.0 copy-start.2
  3.5 1.0 copy-done.2
  4.5 0.0 copy-start.3
  4.5 0.9 copy-done.3
  5.4 0.0 copy-start.4
  5.4 0.9 copy-done.4
  6.4 0.0 copy-start.5
  6.4 0.7 copy-done.5
  7.1 123.8 %shard_map.85 = (bf16[512,512]{1,0:T(8,128)(2,1)S(1)}, bf16[256,1024]{1,0:T(8,128)(2,1)S(1)}, f32[128,1024]{1,0:T(8,128)S(1)}) custom-call(bf16[256,2048]{1,0:T(8,128)(2,1)S(1)} %copy-done.1, f32[1,4096]{1,0:T(1,128)S(1)} %bitcast.1, bf16[512,2048]{1,0:T(8,128)(2,1)S(1)} %copy-done, bf16[256,512]{1,0:T(8,128)(2,1)S(1)} %copy-done.3, ...), custom_call_target="tpu_custom_call" | custom-call | tf_op jit(solution)/shard_map/pallas_call | solution.py:453
  130.9 0.8 copy.12
  131.7 0.8 copy.13
  132.5 0.8 copy.14
Async XLA Ops:
  0.6 1.6 %copy-start = (bf16[512,2048]{1,0:T(8,128)(2,1)S(1)}, bf16[512,2048]{1,0:T(8,128)(2,1)}, u32[]{:S(2)}) copy-start(bf16[512,2048]{1,0:T(8,128)(2,1)} %refs_2_.1) | copy-start | bytes 6291460
  2.2 1.2 copy-start.1
  3.4 1.0 copy-start.2
  4.5 0.9 copy-start.3
  5.4 0.9 copy-start.4
  6.4 0.7 copy-start.5
